TPU v7x, 256 devices: a whole 4x4x8 slice. The times are simulated.
256 devices in a mesh: gx: 8 (over y, core), gy: 32 (over x, z).
Axes of the slice: x: 4, y: 4, z: 8, core: 2. Of those that a mesh axis runs over, the one named last changes fastest.
Arguments:
- control: float32 [1, 2, 6, 1536, 3072], P(None, None, None, 'gy', 'gx'), may hold values from -6 to 6
- sigma: float32 [2, 6, 1536, 3072], P(None, None, 'gy', 'gx'), may hold values from 0.5 to 5
- kappa: float32 [5, 1536, 3072], P(None, 'gy', 'gx'), may hold values from 0.05 to 5
- beta: float32 [6, 1536, 3072], P(None, 'gy', 'gx'), may hold values from -3 to 3
- sea_mask: int32 [1536, 3072], P('gy', 'gx'), may hold values 0 or 1
- x_inverse: float32 [3072, 3072], P('gx'), as said below
- y_inverse: float32 [1536, 1536], P('gx')
- ssh_coef: float32 [2, 6], replicated, may hold values from -1.5 to 1.5
- obs_owner: int32 [65536, 1], P(('gx', 'gy')), may hold values from 0 to 255; in each aligned block of 256 rows (0 to 255, 256 to 511, ...) at most 2 rows name the same one
- tile_index: int32 [65536], P(('gx', 'gy')), may hold values from 0 to 18046, as said below
- obs_frac: float32 [2, 65536], P(None, ('gx', 'gy')), may hold values from 0 to 1
- obs_count: int32 [256], P(('gx', 'gy')), may hold values from 128 to 256
Outputs:
- increments: float32 [1, 2, 6, 1536, 3072], P(None, None, None, 'gy', 'gx')
- sea_height: float32 [1, 1536, 3072], P(None, 'gy', 'gx')
- obs_equiv: float32 [2, 13, 65536], P(None, None, ('gx', 'gy'))
Inputs may be any that keep to these rules, and one draw needn't show every extreme that they name: `obs_owner`: among the slots of one device, at most 2 name the same owner. `tile_index`: row * 384 + column of a cell in the device's own tile, with row below 47 and column below 383. `x_inverse`: the zonal inverse is symmetric.
All inputs are finite; a program needn't handle non-finite values. No bound on the sum of `sea_mask` on one device may be relied on, other than what follows from the above.
Results may differ from a plain program's by a relative error of at most 0.00013.
Values sent between devices are 32-bit elements; how exact they have to be, the bound alone decides.
A program may use at most 128 MiB of HBM per device.

v0:
```python
import jax
import jax.numpy as jnp
from jax import lax
from jax.sharding import PartitionSpec as P

STEPS = 2
CAP = 2


def vertical(values, kappa):
    levels = values.shape[2]
    c_list = []
    d_list = []
    for level in range(levels):
        k_below = kappa[level - 1] if level > 0 else 0.0
        k_above = kappa[level] if level < levels - 1 else 0.0
        diag_term = 1.0 + k_below + k_above
        if level == 0:
            pivot = diag_term
            d_new = values[:, :, 0] / pivot
        else:
            pivot = diag_term + k_below * c_list[-1]
            d_new = (values[:, :, level] + k_below * d_list[-1]) / pivot
        c_list.append(-k_above / pivot)
        d_list.append(d_new)
    result = [d_list[-1]]
    for level in range(levels - 2, -1, -1):
        result.insert(0, d_list[level] - c_list[level] * result[0])
    return jnp.stack(result, axis=2)


def body(
    control,
    sigma,
    kappa,
    beta,
    sea_mask,
    x_inverse,
    y_inverse,
    ssh_coef,
    obs_owner,
    tile_index,
    obs_frac,
    obs_count,
):
    highest = lax.Precision.HIGHEST
    vec_count, kinds, levels, lat_rows, lon_cols = control.shape
    field_count = vec_count * kinds * levels
    sea_open = sea_mask.astype(jnp.float32)
    grid_field = control.reshape(field_count, lat_rows, lon_cols)
    whole_y = lax.all_gather(y_inverse, "gx", axis=0, tiled=True)
    for diffusion_step in range(STEPS):
        grid_field = sea_open * jnp.einsum(
            "fyb,ab->fya",
            lax.all_gather(grid_field, "gx", axis=2, tiled=True),
            x_inverse,
            precision=highest,
        )
        turned = jnp.swapaxes(grid_field, 1, 2)
        merid_lines = lax.all_to_all(turned, "gy", split_axis=1, concat_axis=2, tiled=True)
        solved = jnp.einsum("fxb,ab->fxa", merid_lines, whole_y, precision=highest)
        returned = lax.all_to_all(solved, "gy", split_axis=2, concat_axis=1, tiled=True)
        grid_field = sea_open * jnp.swapaxes(returned, 1, 2)
        grid_field = vertical(
            grid_field.reshape(vec_count, kinds, levels, lat_rows, lon_cols), kappa
        ).reshape(field_count, lat_rows, lon_cols)
    grid_field = grid_field.reshape(vec_count, kinds, levels, lat_rows, lon_cols)
    temper = sigma[0] * grid_field[:, 0]
    saline = sigma[1] * grid_field[:, 1] + beta * temper
    height = jnp.sum(
        ssh_coef[0][None, :, None, None] * temper + ssh_coef[1][None, :, None, None] * saline,
        axis=1,
    )
    increments = jnp.stack([temper, saline], axis=1)
    profile = jnp.concatenate([temper, saline, height[:, None]], axis=1)
    slot_total = tile_index.shape[0]
    row_index = tile_index // lon_cols
    col_index = tile_index % lon_cols
    frac_x = obs_frac[0]
    frac_y = obs_frac[1]
    corner_a = profile[:, :, row_index, col_index]
    corner_b = profile[:, :, row_index, col_index + 1]
    corner_c = profile[:, :, row_index + 1, col_index]
    corner_d = profile[:, :, row_index + 1, col_index + 1]
    interp = (1.0 - frac_y) * ((1.0 - frac_x) * corner_a + frac_x * corner_b) + frac_y * (
        (1.0 - frac_x) * corner_c + frac_x * corner_d
    )
    live_slot = (jnp.arange(slot_total, dtype=jnp.int32) < obs_count[0]).astype(jnp.float32)
    record_len = interp.shape[0] * interp.shape[1]
    interp = (interp * live_slot).reshape(record_len, slot_total)
    gx_count = lax.axis_size("gx")
    gy_count = lax.axis_size("gy")
    device_total = gx_count * gy_count
    owners = obs_owner[:, 0]
    one_hot = (owners[:, None] == jnp.arange(device_total, dtype=jnp.int32)[None, :]).astype(
        jnp.int32
    )
    before = jnp.cumsum(one_hot, axis=0) - one_hot
    slot_rank = jnp.sum(before * one_hot, axis=1)
    outgoing = (
        jnp.zeros((CAP, record_len, device_total), jnp.float32)
        .at[slot_rank, :, owners]
        .set(interp.T)
    )
    outgoing = outgoing.reshape(CAP, record_len, gx_count, gy_count)
    arrived = lax.all_to_all(
        lax.all_to_all(outgoing, "gx", split_axis=2, concat_axis=2, tiled=True),
        "gy",
        split_axis=3,
        concat_axis=3,
        tiled=True,
    )
    obs_equiv = arrived.reshape(CAP, record_len, device_total)
    return (increments, height, obs_equiv)


def solution(mesh):
    return jax.shard_map(
        body,
        mesh=mesh,
        in_specs=(
            P(None, None, None, "gy", "gx"),
            P(None, None, "gy", "gx"),
            P(None, "gy", "gx"),
            P(None, "gy", "gx"),
            P("gy", "gx"),
            P("gx", None),
            P("gx", None),
            P(),
            P(("gx", "gy"), None),
            P(("gx", "gy")),
            P(None, ("gx", "gy")),
            P(("gx", "gy")),
        ),
        out_specs=(
            P(None, None, None, "gy", "gx"),
            P(None, "gy", "gx"),
            P(None, None, ("gx", "gy")),
        ),
        check_vma=False,
    )
```

profile of v0, /device:TPU:1, one launch (start us, length us, event | category | flops | bytes accessed | tf_op | source)
XLA Modules:
  0.0 489.2 jit_solution(15231277766906948029)
XLA Ops:
  9.6 51.3 %all-gather.4.cloned.1.call-done = f32[12,48,3072]{2,1,0:T(8,128)} async-done(((f32[12,48,384]{2,1,0:T(8,128)}), f32[12,48,3072]{2,1,0:T(8,128)}) %all-gather.4.cloned.1.call-update) | async-done | bytes 7077904 | tf_op jit(solution)/shard_map/all_gather | solution.py:55
  60.9 15.1 %fusion.11 = f32[12,384,48]{1,2,0:T(8,128)} fusion(f32[12,48,3072]{2,1,0:T(8,128)} %all-gather.4.cloned.1.call-done, f32[384,3072]{1,0:T(8,128)} %param.17, f32[384,48]{0,1:T(8,128)S(1)} %get-tuple-element.41), kind=kOutput, calls=%fused_computation.16 | convolution fusion | flops 8153948160 | bytes 12754944 | tf_op jit(solution)/shard_map/fyb,ab->fya/dot_general | solution.py:53
  76.0 2.4 copy.92
  78.4 3.3 reshape.729
  81.7 42.5 %all_to_all.82 = f32[32,1,6912]{2,1,0:T(1,128)S(1)} all-to-all(f32[32,1,6912]{2,1,0:T(1,128)} %reshape.729), channel_id=1, replica_groups=mesh['gx'=8,'gy'=32] {'gy'}, dimensions={0} | all-to-all | bytes 1769472 | tf_op jit(solution)/shard_map/all_to_all | solution.py:60
  124.7 3.8 reduce.1
  128.5 2.9 reshape.730
  131.4 2.8 copy.94
  134.2 3.1 all_to_all.61
  137.4 12.0 %fusion.2 = f32[12,12,1536]{2,1,0:T(8,128)S(1)} fusion(f32[12,12,1536]{2,1,0:T(8,128)S(1)} %all_to_all.61, f32[1536,1536]{1,0:T(8,128)} %all-gather.6.cloned.1.call-done), kind=kOutput, calls=%fused_computation.7 | convolution fusion | flops 4076863488 | bytes 11206656 | tf_op jit(solution)/shard_map/fxb,ab->fxa/dot_general | solution.py:61
  149.4 8.6 %copy.95 = f32[12,12,1536]{1,0,2:T(8,128)} copy(f32[12,12,1536]{2,1,0:T(8,128)S(1)} %fusion.2) | data formatting | bytes 1769472 | tf_op jit(solution)/shard_map/fxb,ab->fxa/dot_general | solution.py:61
  158.0 10.0 %reshape.731 = f32[32,1,6912]{2,1,0:T(1,128)} reshape(f32[1536,12,12]{2,1,0:T(8,128)} %bitcast.172) | data formatting | bytes 1769472
  168.0 8.0 %all-to-all-start.1 = ((f32[32,1,6912]{2,1,0:T(1,128)}), f32[32,1,6912]{2,1,0:T(1,128)S(1)}, u32[]{:S(2)}, u32[]{:S(2)}) async-start(f32[32,1,6912]{2,1,0:T(1,128)} %reshape.731), calls=%async_computation.1 | async-start | bytes 1769472 | tf_op jit(solution)/shard_map/all_to_all | solution.py:62
  180.4 17.1 %all-to-all-done.1 = f32[32,1,6912]{2,1,0:T(1,128)S(1)} async-done(((f32[32,1,6912]{2,1,0:T(1,128)}), f32[32,1,6912]{2,1,0:T(1,128)S(1)}, u32[]{:S(2)}, u32[]{:S(2)}) %all-to-all-start.1) | async-done | bytes 884768 | tf_op jit(solution)/shard_map/all_to_all | solution.py:62
  197.4 2.7 reduce.2
  200.2 8.0 %reshape.732 = f32[1536,12,12]{2,1,0:T(8,128)} reshape(f32[32,6912]{1,0:T(8,128)S(1)} %reduce.2) | data formatting | bytes 1769472
  208.2 9.7 %copy.96 = f32[12,12,32,48]{3,1,2,0:T(8,128)S(1)} copy(f32[12,12,32,48]{1,0,3,2:T(8,128)} %bitcast.174) | data formatting | bytes 1769472 | tf_op jit(solution)/shard_map/all_to_all | solution.py:62
  217.9 1.6 all_to_all.65
  219.4 1.8 bitcast_multiply_fusion.1
  225.6 46.7 %all-gather.8.cloned.1.call-done = f32[12,48,3072]{2,1,0:T(8,128)} async-done(((f32[12,48,384]{2,1,0:T(8,128)}), f32[12,48,3072]{2,1,0:T(8,128)}) %all-gather.8.cloned.1.call-update) | async-done | bytes 7077904 | tf_op jit(solution)/shard_map/all_gather | solution.py:55
  272.4 15.1 %fusion.17 = f32[12,384,48]{1,2,0:T(8,128)} fusion(f32[12,48,3072]{2,1,0:T(8,128)} %all-gather.8.cloned.1.call-done, f32[384,3072]{1,0:T(8,128)} %param.17, f32[384,48]{0,1:T(8,128)S(1)} %copy-done.8), kind=kOutput, calls=%fused_computation.18 | convolution fusion | flops 8153948160 | bytes 12754944 | tf_op jit(solution)/shard_map/fyb,ab->fya/dot_general | solution.py:53
  287.5 2.3 copy.98
  289.8 3.3 reshape.733
  293.1 9.7 %all-to-all-start.2 = ((f32[32,1,6912]{2,1,0:T(1,128)}), f32[32,1,6912]{2,1,0:T(1,128)S(1)}, u32[]{:S(2)}, u32[]{:S(2)}) async-start(f32[32,1,6912]{2,1,0:T(1,128)} %reshape.733), calls=%async_computation.2 | async-start | bytes 1769472 | tf_op jit(solution)/shard_map/all_to_all | solution.py:60
  303.9 20.3 %all-to-all-done.2 = f32[32,1,6912]{2,1,0:T(1,128)S(1)} async-done(((f32[32,1,6912]{2,1,0:T(1,128)}), f32[32,1,6912]{2,1,0:T(1,128)S(1)}, u32[]{:S(2)}, u32[]{:S(2)}) %all-to-all-start.2) | async-done | bytes 884768 | tf_op jit(solution)/shard_map/all_to_all | solution.py:60
  324.2 3.8 reduce.3
  328.0 2.9 reshape.734
  330.9 2.8 copy.100
  333.7 3.1 all_to_all.69
  336.8 12.0 %fusion = f32[12,12,1536]{2,1,0:T(8,128)S(1)} fusion(f32[12,12,1536]{2,1,0:T(8,128)S(1)} %all_to_all.69, f32[1536,1536]{1,0:T(8,128)} %all-gather.6.cloned.1.call-done), kind=kOutput, calls=%fused_computation.5 | convolution fusion | flops 4076863488 | bytes 11206656 | tf_op jit(solution)/shard_map/fxb,ab->fxa/dot_general | solution.py:61
  348.8 8.8 %copy.101 = f32[12,12,1536]{1,0,2:T(8,128)} copy(f32[12,12,1536]{2,1,0:T(8,128)S(1)} %fusion) | data formatting | bytes 1769472 | tf_op jit(solution)/shard_map/fxb,ab->fxa/dot_general | solution.py:61
  357.7 10.0 %reshape.735 = f32[32,1,6912]{2,1,0:T(1,128)} reshape(f32[1536,12,12]{2,1,0:T(8,128)} %bitcast.173) | data formatting | bytes 1769472
  367.7 8.4 %all-to-all-start.3 = ((f32[32,1,6912]{2,1,0:T(1,128)}), f32[32,1,6912]{2,1,0:T(1,128)S(1)}, u32[]{:S(2)}, u32[]{:S(2)}) async-start(f32[32,1,6912]{2,1,0:T(1,128)} %reshape.735), calls=%async_computation.3 | async-start | bytes 1769472 | tf_op jit(solution)/shard_map/all_to_all | solution.py:62
  376.5 21.0 %all-to-all-done.3 = f32[32,1,6912]{2,1,0:T(1,128)S(1)} async-done(((f32[32,1,6912]{2,1,0:T(1,128)}), f32[32,1,6912]{2,1,0:T(1,128)S(1)}, u32[]{:S(2)}, u32[]{:S(2)}) %all-to-all-start.3) | async-done | bytes 884768 | tf_op jit(solution)/shard_map/all_to_all | solution.py:62
  397.5 2.8 reduce.4
  400.3 7.6 %reshape.736 = f32[1536,12,12]{2,1,0:T(8,128)} reshape(f32[32,6912]{1,0:T(8,128)S(1)} %reduce.4) | data formatting | bytes 1769472
  407.9 9.7 %copy.102 = f32[12,12,32,48]{3,1,2,0:T(8,128)S(1)} copy(f32[12,12,32,48]{1,0,3,2:T(8,128)} %bitcast.175) | data formatting | bytes 1769472 | tf_op jit(solution)/shard_map/all_to_all | solution.py:62
  419.1 1.9 bitcast_multiply_fusion
  421.9 1.6 subtract_dynamic-update-slice_fusion
  424.9 5.7 %copy.106 = f32[1,13,48,384]{1,3,2,0:T(8,128)} copy(f32[1,13,48,384]{3,2,1,0:T(8,128)S(1)} %pad_maximum_fusion) | data formatting | bytes 1916928 | tf_op jit(solution)/shard_map/concatenate | solution.py:75
  430.6 2.3 gather_fusion.1
  433.0 2.3 gather_fusion.2
  435.4 2.3 gather_fusion.3
  437.8 2.3 gather_fusion
  440.4 12.1 %scatter_fusion = f32[2,13,256]{1,2,0:T(8,128)S(1)} fusion(f32[2,13,256]{1,2,0:T(8,128)S(1)} %broadcast_in_dim.15, s32[256]{0:T(256)S(1)} %bitcast.176, f32[256,13]{1,0:T(8,128)S(1)} %copy.111), kind=kCustom, calls=%fused_computation.4 | custom fusion | bytes 41984 | tf_op jit(solution)/shard_map/scatter | solution.py:103
  452.8 12.6 %all_to_all.83 = f32[8,1,832]{2,1,0:T(1,128)S(1)} all-to-all(f32[8,1,832]{2,1,0:T(1,128)S(1)} %reshape.737), channel_id=1, replica_groups=mesh['gx'=8,'gy'=32] {'gx'}, dimensions={0} | all-to-all | bytes 53248 | tf_op jit(solution)/shard_map/all_to_all | solution.py:107
  467.2 4.5 all-to-all-start.5
  472.7 7.8 %all-to-all-done.5 = f32[32,1,208]{2,1,0:T(1,128)S(1)} async-done(((f32[32,1,208]{2,1,0:T(1,128)}), f32[32,1,208]{2,1,0:T(1,128)S(1)}, u32[]{:S(2)}, u32[]{:S(2)}) %all-to-all-start.5) | async-done | bytes 26656 | tf_op jit(solution)/shard_map/all_to_all | solution.py:106
  (97 shorter events, 21.4 us)
Async XLA Ops:
  7.2 53.7 %all-gather.4.cloned.1.call-start = ((), (), s32[]{:S(2)}) async-start(), calls=%async_computation.6 | async-start | bytes 7962624 | tf_op jit(solution)/shard_map/all_gather | solution.py:55
  7.9 129.5 %all-gather.6.cloned.1.call-start = ((), (), s32[]{:S(2)}) async-start(), calls=%async_computation.7 | async-start | bytes 10616832 | tf_op jit(solution)/shard_map/all_gather | solution.py:51
  9.5 51.3 %copy-start.7 = (f32[384,48]{0,1:T(8,128)}, f32[384,48]{0,1:T(8,128)S(1)}, u32[]{:S(2)}) copy-start(f32[384,48]{0,1:T(8,128)S(1)} %get-tuple-element.41) | copy-start | bytes 221188
  158.0 18.9 %copy-start = (f32[5,48,384]{2,1,0:T(8,128)S(1)}, f32[5,48,384]{2,1,0:T(8,128)}, u32[]{:S(2)}) copy-start(f32[5,48,384]{2,1,0:T(8,128)} %param.14) | copy-start | bytes 1105924
  168.0 29.5 %all-to-all-start.1 = ((f32[32,1,6912]{2,1,0:T(1,128)}), f32[32,1,6912]{2,1,0:T(1,128)S(1)}, u32[]{:S(2)}, u32[]{:S(2)}) async-start(f32[32,1,6912]{2,1,0:T(1,128)} %reshape.731), calls=%async_computation.1 | async-start | bytes 1769472 | tf_op jit(solution)/shard_map/all_to_all | solution.py:62
  176.0 96.3 %all-gather.8.cloned.1.call-start = ((), (), s32[]{:S(2)}) async-start(), calls=%async_computation.8 | async-start | bytes 7962624 | tf_op jit(solution)/shard_map/all_gather | solution.py:55
  177.6 2.8 copy-start.3
  178.3 0.6 copy-start.2
  222.2 50.2 %copy-start.8 = (f32[384,48]{0,1:T(8,128)S(1)}, f32[384,48]{0,1:T(8,128)}, u32[]{:S(2)}) copy-start(f32[384,48]{0,1:T(8,128)} %copy-done.7) | copy-start | bytes 221188
  224.7 0.9 copy-start.1
  287.5 16.0 %copy-start.11 = (s32[256,1]{0,1:T(1,128)S(1)}, s32[256,1]{0,1:T(1,128)}, u32[]{:S(2)}) copy-start(s32[256,1]{0,1:T(1,128)} %param.20) | copy-start | bytes 3076
  293.1 31.1 %all-to-all-start.2 = ((f32[32,1,6912]{2,1,0:T(1,128)}), f32[32,1,6912]{2,1,0:T(1,128)S(1)}, u32[]{:S(2)}, u32[]{:S(2)}) async-start(f32[32,1,6912]{2,1,0:T(1,128)} %reshape.733), calls=%async_computation.2 | async-start | bytes 1769472 | tf_op jit(solution)/shard_map/all_to_all | solution.py:60
  303.8 20.4 %copy-start.4 = (s32[256,2,128]{0,1,2:T(2,128)}, s32[256,2,128]{0,1,2:T(2,128)S(1)}, u32[]{:S(2)}) copy-start(s32[256,2,128]{0,1,2:T(2,128)S(1)} %fusion.23) | copy-start | bytes 786436
  303.9 29.8 %copy-start.12 = (s32[256,3]{0,1:T(4,128)}, s32[256,3]{0,1:T(4,128)S(1)}, u32[]{:S(2)}) copy-start(s32[256,3]{0,1:T(4,128)S(1)} %reduce-window.9) | copy-start | bytes 9220
  357.7 18.4 %slice-start = ((s32[256,3]{0,1:T(4,128)}), s32[256,2]{0,1:T(2,128)S(1)}, s32[]{:S(2)}) async-start(s32[256,3]{0,1:T(4,128)} %copy-done.12), calls=%async_computation.9 | async-start | bytes 4096 | tf_op jit(solution)/shard_map/slice.1
  357.7 18.4 %copy-start.5 = (s32[256,2,128]{0,1,2:T(2,128)S(1)}, s32[256,2,128]{0,1,2:T(2,128)}, u32[]{:S(2)}) copy-start(s32[256,2,128]{0,1,2:T(2,128)} %copy-done.4) | copy-start | bytes 786436
  357.7 18.7 %copy-start.15 = (f32[2,6]{1,0:T(2,128)S(1)}, f32[2,6]{1,0:T(2,128)}, u32[]{:S(2)}) copy-start(f32[2,6]{1,0:T(2,128)} %param.19) | copy-start | bytes 148
  357.7 18.7 %copy-start.13 = (s32[256]{0:T(256)S(1)}, s32[256]{0:T(256)}, u32[]{:S(2)}) copy-start(s32[256]{0:T(256)} %param.21) | copy-start | bytes 3076
  357.7 18.7 %copy-start.14 = (f32[2,256]{1,0:T(2,128)S(1)}, f32[2,256]{1,0:T(2,128)}, u32[]{:S(2)}) copy-start(f32[2,256]{1,0:T(2,128)} %param.22) | copy-start | bytes 6148
  367.7 29.8 %all-to-all-start.3 = ((f32[32,1,6912]{2,1,0:T(1,128)}), f32[32,1,6912]{2,1,0:T(1,128)S(1)}, u32[]{:S(2)}, u32[]{:S(2)}) async-start(f32[32,1,6912]{2,1,0:T(1,128)} %reshape.735), calls=%async_computation.3 | async-start | bytes 1769472 | tf_op jit(solution)/shard_map/all_to_all | solution.py:62
  421.9 2.6 copy-start.6
  421.9 2.6 copy-start.9
  424.8 5.8 %copy-start.10 = (f32[48,384]{1,0:T(8,128)}, f32[48,384]{1,0:T(8,128)S(1)}, u32[]{:S(2)}) copy-start(f32[48,384]{1,0:T(8,128)S(1)} %get-tuple-element.11) | copy-start | bytes 221188
  467.2 13.2 %all-to-all-start.5 = ((f32[32,1,208]{2,1,0:T(1,128)}), f32[32,1,208]{2,1,0:T(1,128)S(1)}, u32[]{:S(2)}, u32[]{:S(2)}) async-start(f32[32,1,208]{2,1,0:T(1,128)} %reshape.739), calls=%async_computation.5 | async-start | bytes 65536 | tf_op jit(solution)/shard_map/all_to_all | solution.py:106
Sparse Core Ops, SparseCore 0:
  9.8 51.0 all-gather.3
  62.7 56.8 all-gather.5
  225.8 46.5 all-gather.7
where the time goes:
time: 498 us; the launch traced here: 489 us
  waiting for transfers between devices  166 us (33%)
  local copies, waits for them, and re-layouts  140 us (28%)
  blocking collectives  55.1 us (11%)
  matrix products  54.3 us (11%)
  starting transfers between devices  30.7 us (6%)
  other arithmetic  28 us (6%)
  between operations  15.3 us (3%)
    all_gather x2, waiting for transfers between devices, body(): lax.all_gather(grid_field, 'gx', axis=2, tiled=True)  98 us
    unnamed x49, local copies, waits for them, and re-layouts  50.9 us
    all_to_all x1, blocking collectives, body(): lax.all_to_all(turned, 'gy', split_axis=1, concat_axis=2, tiled=True)  42.5 us
    all_to_all x2, waiting for transfers between devices, body(): lax.all_to_all(solved, 'gy', split_axis=2, concat_axis=1, tiled=True)  38.1 us
    dot_general x2, matrix products, body(): jnp.einsum('fyb,ab->fya', lax.all_gather(grid_field, 'gx', axis=2, tiled=...  30.3 us
    dot_general x2, matrix products, body(): solved = jnp.einsum('fxb,ab->fxa', merid_lines, whole_y, precision=highest)  24 us
    all_to_all x4, local copies, waits for them, and re-layouts, body(): lax.all_to_all(solved, 'gy', split_axis=2, concat_axis=1, tiled=True)  22.5 us
    all_to_all x1, waiting for transfers between devices, body(): lax.all_to_all(turned, 'gy', split_axis=1, concat_axis=2, tiled=True)  20.3 us
  transfers between devices with their start and end apart: 7, of which 6 were waited for; matrix products, arithmetic and copies ran while one was open for 8% of the time, Pallas kernels for 0%

commit v1 on v0

--- a/solution.py
+++ b/solution.py
@@ -59,7 +59,12 @@
         turned = jnp.swapaxes(grid_field, 1, 2)
         merid_lines = lax.all_to_all(turned, "gy", split_axis=1, concat_axis=2, tiled=True)
         solved = jnp.einsum("fxb,ab->fxa", merid_lines, whole_y, precision=highest)
-        returned = lax.all_to_all(solved, "gy", split_axis=2, concat_axis=1, tiled=True)
+        returned = jnp.concatenate(
+            jax.lax.all_to_all(
+                jnp.stack(jnp.split(solved, jax.lax.axis_size("gy"), axis=2), 0), "gy", 0, 0
+            ),
+            1,
+        )
         grid_field = sea_open * jnp.swapaxes(returned, 1, 2)
         grid_field = vertical(
             grid_field.reshape(vec_count, kinds, levels, lat_rows, lon_cols), kappa

time: 498 us -> 442 us (0.89)
  local copies, waits for them, and re-layouts: 140 us -> 94.9 us
  blocking collectives: 55.1 us -> 44.3 us
    all_to_all x4 -> x0, local copies, waits for them, and re-layouts: 22.5 us -> none  [body(): lax.all_to_all(solved, 'gy', split_axis=2, concat_axis=1, tiled=True)]
    unnamed x49 -> x119, local copies, waits for them, and re-layouts: 50.9 us -> 32.7 us
    dot_general x2 -> x0, local copies, waits for them, and re-layouts: 17.5 us -> none  [body(): solved = jnp.einsum('fxb,ab->fxa', merid_lines, whole_y, precision=highest)]
    reshape x0 -> x4, local copies, waits for them, and re-layouts: none -> 11.9 us  [body(): jnp.concatenate(jax.lax.all_to_all(jnp.stack(jnp.split(solved, jax.lax.ax...]
    all_to_all x1, blocking collectives: 42.5 us -> 31.8 us  [body(): lax.all_to_all(turned, 'gy', split_axis=1, concat_axis=2, tiled=True)]
  transfers between devices with their start and end apart: 7 -> 7, of which waited for: 6 -> 6; matrix products, arithmetic and copies ran while one was open for 8% -> 9% of each run, Pallas kernels for 0% -> 0%
where the time goes in v1:
time: 442 us; the launch traced here: 433 us
  waiting for transfers between devices  162 us (37%)
  local copies, waits for them, and re-layouts  94.9 us (21%)
  matrix products  54.4 us (12%)
  blocking collectives  44.3 us (10%)
  starting transfers between devices  31.1 us (7%)
  other arithmetic  30.5 us (7%)
  between operations  15.6 us (4%)
    all_gather x2, waiting for transfers between devices, body(): lax.all_gather(grid_field, 'gx', axis=2, tiled=True)  97.4 us
    all_to_all x2, waiting for transfers between devices, body(): jax.lax.all_to_all(jnp.stack(jnp.split(solved, jax.lax.axis_size('gy'), a...  35.3 us
    unnamed x119, local copies, waits for them, and re-layouts  32.7 us
    all_to_all x1, blocking collectives, body(): lax.all_to_all(turned, 'gy', split_axis=1, concat_axis=2, tiled=True)  31.8 us
    dot_general x2, matrix products, body(): jnp.einsum('fyb,ab->fya', lax.all_gather(grid_field, 'gx', axis=2, tiled=...  30.3 us
    dot_general x2, matrix products, body(): solved = jnp.einsum('fxb,ab->fxa', merid_lines, whole_y, precision=highest)  24.1 us
    all_to_all x1, waiting for transfers between devices, body(): lax.all_to_all(turned, 'gy', split_axis=1, concat_axis=2, tiled=True)  20.3 us
    all_to_all x2, starting transfers between devices, body(): jax.lax.all_to_all(jnp.stack(jnp.split(solved, jax.lax.axis_size('gy'), a...  16.6 us
  transfers between devices with their start and end apart: 7, of which 6 were waited for; matrix products, arithmetic and copies ran while one was open for 9% of the time, Pallas kernels for 0%

profile of v1, /device:TPU:1, one launch (start us, length us, event | category | flops | bytes accessed | tf_op | source)
XLA Modules:
  0.0 433.2 jit_solution(551888291459447017)
XLA Ops:
  10.2 50.7 %all-gather.4.cloned.1.call-done = f32[12,48,3072]{2,1,0:T(8,128)} async-done(((f32[12,48,384]{2,1,0:T(8,128)}), f32[12,48,3072]{2,1,0:T(8,128)}) %all-gather.4.cloned.1.call-update) | async-done | bytes 7077904 | tf_op jit(solution)/shard_map/all_gather | solution.py:55
  60.9 15.1 %fusion.11 = f32[12,384,48]{1,2,0:T(8,128)} fusion(f32[12,48,3072]{2,1,0:T(8,128)} %all-gather.4.cloned.1.call-done, f32[384,3072]{1,0:T(8,128)} %param.17, f32[384,48]{0,1:T(8,128)S(1)} %get-tuple-element.41), kind=kOutput, calls=%fused_computation.16 | convolution fusion | flops 8153948160 | bytes 12754944 | tf_op jit(solution)/shard_map/fyb,ab->fya/dot_general | solution.py:53
  76.0 2.4 copy.88
  78.4 3.3 reshape.745
  81.7 31.8 %all_to_all.56 = f32[32,1,6912]{2,1,0:T(1,128)S(1)} all-to-all(f32[32,1,6912]{2,1,0:T(1,128)} %reshape.745), channel_id=1, replica_groups=mesh['gx'=8,'gy'=32] {'gy'}, dimensions={0} | all-to-all | bytes 1769472 | tf_op jit(solution)/shard_map/all_to_all | solution.py:60
  113.9 3.7 reduce.1
  117.6 3.0 reshape.746
  120.6 2.8 copy.90
  123.4 3.1 all_to_all.41
  126.5 12.2 %fusion.2 = f32[12,12,1536]{2,1,0:T(8,128)S(1)} fusion(f32[12,12,1536]{2,1,0:T(8,128)S(1)} %all_to_all.41, f32[1536,1536]{1,0:T(8,128)} %all-gather.6.cloned.1.call-done), kind=kOutput, calls=%fused_computation.7 | convolution fusion | flops 4076863488 | bytes 11206656 | tf_op jit(solution)/shard_map/fxb,ab->fxa/dot_general | solution.py:61
  141.4 3.3 reshape.747
  144.7 8.1 %all-to-all-start.1 = ((f32[32,1,6912]{2,1,0:T(1,128)}), f32[32,1,6912]{2,1,0:T(1,128)S(1)}, u32[]{:S(2)}, u32[]{:S(2)}) async-start(f32[32,1,6912]{2,1,0:T(1,128)} %reshape.747), calls=%async_computation.1 | async-start | bytes 1769472 | tf_op jit(solution)/shard_map/all_to_all | solution.py:63
  152.9 1.7 copy.87
  155.3 1.7 multiply_add_fusion
  159.0 15.3 %all-to-all-done.1 = f32[32,1,6912]{2,1,0:T(1,128)S(1)} async-done(((f32[32,1,6912]{2,1,0:T(1,128)}), f32[32,1,6912]{2,1,0:T(1,128)S(1)}, u32[]{:S(2)}, u32[]{:S(2)}) %all-to-all-start.1) | async-done | bytes 884768 | tf_op jit(solution)/shard_map/all_to_all | solution.py:63
  174.2 3.7 reduce.2
  177.9 3.1 reshape.748
  181.0 2.0 copy.91
  183.0 4.0 reshape.664
  187.0 1.8 bitcast_multiply_fusion.1
  192.4 46.7 %all-gather.8.cloned.1.call-done = f32[12,48,3072]{2,1,0:T(8,128)} async-done(((f32[12,48,384]{2,1,0:T(8,128)}), f32[12,48,3072]{2,1,0:T(8,128)}) %all-gather.8.cloned.1.call-update) | async-done | bytes 7077904 | tf_op jit(solution)/shard_map/all_gather | solution.py:55
  239.1 15.1 %fusion.17 = f32[12,384,48]{1,2,0:T(8,128)} fusion(f32[12,48,3072]{2,1,0:T(8,128)} %all-gather.8.cloned.1.call-done, f32[384,3072]{1,0:T(8,128)} %param.17, f32[384,48]{0,1:T(8,128)S(1)} %copy-done.12), kind=kOutput, calls=%fused_computation.18 | convolution fusion | flops 8153948160 | bytes 12754944 | tf_op jit(solution)/shard_map/fyb,ab->fya/dot_general | solution.py:53
  254.2 2.3 copy.93
  256.5 3.3 reshape.749
  259.8 10.0 %all-to-all-start.2 = ((f32[32,1,6912]{2,1,0:T(1,128)}), f32[32,1,6912]{2,1,0:T(1,128)S(1)}, u32[]{:S(2)}, u32[]{:S(2)}) async-start(f32[32,1,6912]{2,1,0:T(1,128)} %reshape.749), calls=%async_computation.2 | async-start | bytes 1769472 | tf_op jit(solution)/shard_map/all_to_all | solution.py:60
  270.9 20.3 %all-to-all-done.2 = f32[32,1,6912]{2,1,0:T(1,128)S(1)} async-done(((f32[32,1,6912]{2,1,0:T(1,128)}), f32[32,1,6912]{2,1,0:T(1,128)S(1)}, u32[]{:S(2)}, u32[]{:S(2)}) %all-to-all-start.2) | async-done | bytes 884768 | tf_op jit(solution)/shard_map/all_to_all | solution.py:60
  291.2 3.7 reduce.3
  294.9 2.9 reshape.750
  297.8 2.8 copy.95
  300.6 3.1 all_to_all.46
  303.7 12.0 %fusion = f32[12,12,1536]{2,1,0:T(8,128)S(1)} fusion(f32[12,12,1536]{2,1,0:T(8,128)S(1)} %all_to_all.46, f32[1536,1536]{1,0:T(8,128)} %all-gather.6.cloned.1.call-done), kind=kOutput, calls=%fused_computation.5 | convolution fusion | flops 4076863488 | bytes 11206656 | tf_op jit(solution)/shard_map/fxb,ab->fxa/dot_general | solution.py:61
  318.5 3.3 reshape.751
  321.8 8.5 %all-to-all-start.3 = ((f32[32,1,6912]{2,1,0:T(1,128)}), f32[32,1,6912]{2,1,0:T(1,128)S(1)}, u32[]{:S(2)}, u32[]{:S(2)}) async-start(f32[32,1,6912]{2,1,0:T(1,128)} %reshape.751), calls=%async_computation.3 | async-start | bytes 1769472 | tf_op jit(solution)/shard_map/all_to_all | solution.py:63
  331.7 20.1 %all-to-all-done.3 = f32[32,1,6912]{2,1,0:T(1,128)S(1)} async-done(((f32[32,1,6912]{2,1,0:T(1,128)}), f32[32,1,6912]{2,1,0:T(1,128)S(1)}, u32[]{:S(2)}, u32[]{:S(2)}) %all-to-all-start.3) | async-done | bytes 884768 | tf_op jit(solution)/shard_map/all_to_all | solution.py:63
  351.7 3.8 reduce.4
  355.5 2.9 reshape.752
  358.4 1.9 copy.96
  360.3 4.0 reshape.668
  364.3 1.9 bitcast_multiply_fusion
  369.2 5.7 %copy.100 = f32[1,13,48,384]{1,3,2,0:T(8,128)} copy(f32[1,13,48,384]{3,2,1,0:T(8,128)S(1)} %pad_maximum_fusion) | data formatting | bytes 1916928 | tf_op jit(solution)/shard_map/concatenate | solution.py:80
  374.9 2.3 gather_fusion.1
  377.3 2.3 gather_fusion.2
  379.7 2.3 gather_fusion.3
  382.1 2.3 gather_fusion
  384.7 12.1 %scatter_fusion = f32[2,13,256]{1,2,0:T(8,128)S(1)} fusion(f32[2,13,256]{1,2,0:T(8,128)S(1)} %broadcast_in_dim.15, s32[256]{0:T(256)S(1)} %bitcast.422, f32[256,13]{1,0:T(8,128)S(1)} %copy.105), kind=kCustom, calls=%fused_computation.4 | custom fusion | bytes 41984 | tf_op jit(solution)/shard_map/scatter | solution.py:108
  397.2 12.6 %all_to_all.57 = f32[8,1,832]{2,1,0:T(1,128)S(1)} all-to-all(f32[8,1,832]{2,1,0:T(1,128)S(1)} %reshape.753), channel_id=1, replica_groups=mesh['gx'=8,'gy'=32] {'gx'}, dimensions={0} | all-to-all | bytes 53248 | tf_op jit(solution)/shard_map/all_to_all | solution.py:112
  411.5 4.4 %all-to-all-start.5 = ((f32[32,1,208]{2,1,0:T(1,128)}), f32[32,1,208]{2,1,0:T(1,128)S(1)}, u32[]{:S(2)}, u32[]{:S(2)}) async-start(f32[32,1,208]{2,1,0:T(1,128)} %reshape.755), calls=%async_computation.5 | async-start | bytes 65536 | tf_op jit(solution)/shard_map/all_to_all | solution.py:111
  416.9 7.8 %all-to-all-done.5 = f32[32,1,208]{2,1,0:T(1,128)S(1)} async-done(((f32[32,1,208]{2,1,0:T(1,128)}), f32[32,1,208]{2,1,0:T(1,128)S(1)}, u32[]{:S(2)}, u32[]{:S(2)}) %all-to-all-start.5) | async-done | bytes 26656 | tf_op jit(solution)/shard_map/all_to_all | solution.py:111
  (167 shorter events, 24.5 us)
Async XLA Ops:
  7.2 53.7 %all-gather.4.cloned.1.call-start = ((), (), s32[]{:S(2)}) async-start(), calls=%async_computation.6 | async-start | bytes 7962624 | tf_op jit(solution)/shard_map/all_gather | solution.py:55
  7.9 118.6 %all-gather.6.cloned.1.call-start = ((), (), s32[]{:S(2)}) async-start(), calls=%async_computation.7 | async-start | bytes 10616832 | tf_op jit(solution)/shard_map/all_gather | solution.py:51
  10.2 50.7 %copy-start.11 = (f32[384,48]{0,1:T(8,128)}, f32[384,48]{0,1:T(8,128)S(1)}, u32[]{:S(2)}) copy-start(f32[384,48]{0,1:T(8,128)S(1)} %get-tuple-element.41) | copy-start | bytes 221188
  141.3 13.2 %copy-start = (f32[5,48,384]{2,1,0:T(8,128)S(1)}, f32[5,48,384]{2,1,0:T(8,128)}, u32[]{:S(2)}) copy-start(f32[5,48,384]{2,1,0:T(8,128)} %param.14) | copy-start | bytes 1105924
  144.7 12.8 %copy-start.1 = (f32[5,48,384]{2,1,0:T(8,128)S(1)}, f32[5,48,384]{2,1,0:T(8,128)}, u32[]{:S(2)}) copy-start(f32[5,48,384]{2,1,0:T(8,128)} %param.14) | copy-start | bytes 1105924
  144.7 29.5 %all-to-all-start.1 = ((f32[32,1,6912]{2,1,0:T(1,128)}), f32[32,1,6912]{2,1,0:T(1,128)S(1)}, u32[]{:S(2)}, u32[]{:S(2)}) async-start(f32[32,1,6912]{2,1,0:T(1,128)} %reshape.747), calls=%async_computation.1 | async-start | bytes 1769472 | tf_op jit(solution)/shard_map/all_to_all | solution.py:63
  152.8 86.2 %all-gather.8.cloned.1.call-start = ((), (), s32[]{:S(2)}) async-start(), calls=%async_computation.8 | async-start | bytes 7962624 | tf_op jit(solution)/shard_map/all_gather | solution.py:55
  155.3 19.0 %copy-start.8 = (f32[48,384]{1,0:T(8,128)}, f32[48,384]{1,0:T(8,128)S(1)}, u32[]{:S(2)}) copy-start(f32[48,384]{1,0:T(8,128)S(1)} %get-tuple-element.25) | copy-start | bytes 221188
  157.0 0.6 copy-start.7
  183.0 4.0 copy-start.4
  189.7 1.5 copy-start.2
  189.7 49.3 %copy-start.12 = (f32[384,48]{0,1:T(8,128)S(1)}, f32[384,48]{0,1:T(8,128)}, u32[]{:S(2)}) copy-start(f32[384,48]{0,1:T(8,128)} %copy-done.11) | copy-start | bytes 221188
  191.4 0.9 copy-start.6
  256.5 14.0 %copy-start.15 = (s32[256,1]{0,1:T(1,128)S(1)}, s32[256,1]{0,1:T(1,128)}, u32[]{:S(2)}) copy-start(s32[256,1]{0,1:T(1,128)} %param.20) | copy-start | bytes 3076
  259.8 31.4 %all-to-all-start.2 = ((f32[32,1,6912]{2,1,0:T(1,128)}), f32[32,1,6912]{2,1,0:T(1,128)S(1)}, u32[]{:S(2)}, u32[]{:S(2)}) async-start(f32[32,1,6912]{2,1,0:T(1,128)} %reshape.749), calls=%async_computation.2 | async-start | bytes 1769472 | tf_op jit(solution)/shard_map/all_to_all | solution.py:60
  270.8 20.4 %copy-start.9 = (s32[256,2,128]{0,1,2:T(2,128)}, s32[256,2,128]{0,1,2:T(2,128)S(1)}, u32[]{:S(2)}) copy-start(s32[256,2,128]{0,1,2:T(2,128)S(1)} %fusion.23) | copy-start | bytes 786436
  270.9 29.7 %copy-start.16 = (s32[256,3]{0,1:T(4,128)}, s32[256,3]{0,1:T(4,128)S(1)}, u32[]{:S(2)}) copy-start(s32[256,3]{0,1:T(4,128)S(1)} %reduce-window.9) | copy-start | bytes 9220
  318.2 12.1 %slice-start = ((s32[256,3]{0,1:T(4,128)}), s32[256,2]{0,1:T(2,128)S(1)}, s32[]{:S(2)}) async-start(s32[256,3]{0,1:T(4,128)} %copy-done.16), calls=%async_computation.9 | async-start | bytes 4096 | tf_op jit(solution)/shard_map/slice.1
  318.4 13.1 %copy-start.19 = (f32[2,6]{1,0:T(2,128)S(1)}, f32[2,6]{1,0:T(2,128)}, u32[]{:S(2)}) copy-start(f32[2,6]{1,0:T(2,128)} %param.19) | copy-start | bytes 148
  318.5 13.1 %copy-start.17 = (s32[256]{0:T(256)S(1)}, s32[256]{0:T(256)}, u32[]{:S(2)}) copy-start(s32[256]{0:T(256)} %param.21) | copy-start | bytes 3076
  318.5 13.2 %copy-start.18 = (f32[2,256]{1,0:T(2,128)S(1)}, f32[2,256]{1,0:T(2,128)}, u32[]{:S(2)}) copy-start(f32[2,256]{1,0:T(2,128)} %param.22) | copy-start | bytes 6148
  321.8 30.0 %all-to-all-start.3 = ((f32[32,1,6912]{2,1,0:T(1,128)}), f32[32,1,6912]{2,1,0:T(1,128)S(1)}, u32[]{:S(2)}, u32[]{:S(2)}) async-start(f32[32,1,6912]{2,1,0:T(1,128)} %reshape.751), calls=%async_computation.3 | async-start | bytes 1769472 | tf_op jit(solution)/shard_map/all_to_all | solution.py:63
  360.3 4.0 copy-start.5
  367.1 1.6 copy-start.3
  367.1 1.8 copy-start.10
  367.1 1.8 copy-start.13
  369.1 5.8 %copy-start.14 = (f32[48,384]{1,0:T(8,128)}, f32[48,384]{1,0:T(8,128)S(1)}, u32[]{:S(2)}) copy-start(f32[48,384]{1,0:T(8,128)S(1)} %get-tuple-element.11) | copy-start | bytes 221188
  411.5 13.2 %all-to-all-start.5 = ((f32[32,1,208]{2,1,0:T(1,128)}), f32[32,1,208]{2,1,0:T(1,128)S(1)}, u32[]{:S(2)}, u32[]{:S(2)}) async-start(f32[32,1,208]{2,1,0:T(1,128)} %reshape.755), calls=%async_computation.5 | async-start | bytes 65536 | tf_op jit(solution)/shard_map/all_to_all | solution.py:111
Sparse Core Ops, SparseCore 0:
  9.8 51.0 all-gather.3
  62.7 56.8 all-gather.5
  192.5 46.5 all-gather.7
